TPU v7x, 32 devices: a whole 2x2x4 slice. The times are simulated.
32 devices in a mesh: copies: 2 (over y), blk: 4 (over x, core), virt: 4 (over z).
Axes of the slice: x: 2, y: 2, z: 4, core: 2. Of those that a mesh axis runs over, the one named last changes fastest.
Arguments:
- three_index: bfloat16 [32, 512, 2048], P(('copies', 'blk'), 'virt'), parts along dimension 0, may hold values from -0.59765625 to 0.59765625
- occ_energy: float32 [32], P(('copies', 'blk')), parts along dimension 0, may hold values from -2 to -0.5
- virt_energy: float32 [1024], P('copies'), parts along dimension 0, may hold values from 0.3 to 3
Outputs:
- gradient: bfloat16 [32, 512, 2048], P(('copies', 'blk'), 'virt'), parts along dimension 0
There are 2 independent parts, one for each index of `copies`. A program takes and returns all parts, laid end to end along the dimension named above; each array names one. Nothing has to cross between parts.
All inputs are finite; a program needn't handle non-finite values.
Results may differ from a plain program's by a relative error of at most 0.0055.
Values may be sent and summed in bfloat16 or wider, within the bound.
A program may use at most 64 MiB of HBM per device.

v0:
```python
import jax
import jax.numpy as jnp
from jax import lax
from jax.sharding import PartitionSpec as P


def shifted(shard, axis, by):
    devices = lax.axis_size(axis)
    return lax.ppermute(shard, axis, [(i, (i + by) % devices) for i in range(devices)])


def contract(left, right):
    return lax.dot_general(
        left, right, (((1,), (1,)), ((), ())), preferred_element_type=jnp.float32
    )


def pair_block(
    own_rows,
    part_full,
    part_rows,
    own_full,
    energy_own,
    energy_part,
    energy_rows,
    virt_energy,
    diagonal,
):
    occ_count, rows_here, aux_count = own_rows.shape
    virt_count = part_full.shape[1]
    first = contract(
        own_rows.reshape(occ_count * rows_here, aux_count),
        part_full.reshape(occ_count * virt_count, aux_count),
    )
    first = first.reshape(occ_count, rows_here, occ_count, virt_count)
    if diagonal:
        second = first.transpose(2, 1, 0, 3)
    else:
        second = contract(
            part_rows.reshape(occ_count * rows_here, aux_count),
            own_full.reshape(occ_count * virt_count, aux_count),
        )
        second = second.reshape(occ_count, rows_here, occ_count, virt_count).transpose(2, 1, 0, 3)
    denom = (
        energy_own[:, None, None, None]
        + energy_part[None, None, :, None]
        - energy_rows[None, :, None, None]
        - virt_energy[None, None, None, :]
    )
    tbar = ((2.0 * first - second) / denom).astype(jnp.bfloat16)
    flat = tbar.reshape(occ_count * rows_here, occ_count * virt_count)
    own = jnp.dot(
        flat,
        part_full.reshape(occ_count * virt_count, aux_count),
        preferred_element_type=jnp.float32,
    )
    return (tbar, first, own.reshape(occ_count, rows_here, aux_count))


def local(three_index, occ_energy, virt_energy):
    occ_count, rows_here, aux_count = three_index.shape
    virt_count = virt_energy.shape[0]
    row_start = lax.axis_index("virt") * rows_here
    energy_rows = lax.dynamic_slice_in_dim(virt_energy, row_start, rows_here, 0)
    own_full = lax.all_gather(three_index, "virt", axis=1, tiled=True)
    part_full, energy_part = (
        shifted(own_full, "blk", 1),
        shifted(occ_energy.astype(jnp.bfloat16), "blk", 1).astype(occ_energy.dtype),
    )
    part_rows = lax.dynamic_slice_in_dim(part_full, row_start, rows_here, 1)
    unused_tbar, unused_first, diag_own = pair_block(
        three_index,
        own_full,
        three_index,
        own_full,
        occ_energy,
        occ_energy,
        energy_rows,
        virt_energy,
        True,
    )
    tbar, first, cross_own = pair_block(
        three_index,
        part_full,
        part_rows,
        own_full,
        occ_energy,
        energy_part,
        energy_rows,
        virt_energy,
        False,
    )
    tiles = lax.all_to_all(tbar, "virt", split_axis=3, concat_axis=1, tiled=True)
    partial_value = lax.dot_general(
        tiles.reshape(occ_count * virt_count, occ_count * rows_here),
        own_full.reshape(occ_count * virt_count, aux_count),
        (((0,), (0,)), ((), ())),
        preferred_element_type=jnp.float32,
    )
    summed = partial_value.reshape(occ_count, rows_here, aux_count).astype(jnp.bfloat16)
    partner = shifted(summed, "blk", -1)
    return (diag_own + cross_own + partner.astype(jnp.float32)).astype(jnp.bfloat16)


def solution(mesh):
    placed = (P(("copies", "blk"), "virt", None), P(("copies", "blk")), P("copies"))
    return jax.shard_map(
        local,
        mesh=mesh,
        in_specs=placed,
        out_specs=P(("copies", "blk"), "virt", None),
        check_vma=False,
    )
```

profile of v0, /device:TPU:1, one launch (start us, length us, event | category | flops | bytes accessed | tf_op | source)
XLA Modules:
  0.0 382.6 jit_solution(1829108738289670631)
XLA Ops:
  6.5 0.0 all-gather.2.cloned.1.call-start
  6.5 0.7 all-gather.2.cloned.1.call-update
  7.3 153.5 %all-gather.2.cloned.1.call-done = bf16[4,512,2048]{2,1,0:T(8,128)(2,1)} async-done(((bf16[4,128,2048]{2,1,0:T(8,128)(2,1)}), bf16[4,512,2048]{2,1,0:T(8,128)(2,1)}) %all-gather.2.cloned.1.call-update) | async-done | bytes 8388624 | tf_op jit(solution)/shard_map/all_gather | solution.py:65
  160.8 1.6 collective-permute-start
  162.4 0.7 convert_element_type.22
  163.0 0.0 collective-permute-start.1
  163.0 0.8 dynamic_slice.6
  163.8 89.3 %collective-permute-done.1 = bf16[4]{0:T(256)(128)(2,1)S(1)} collective-permute-done((bf16[4]{0:T(256)(128)(2,1)S(1)}, bf16[4]{0:T(256)(128)(2,1)S(1)}, u32[]{:S(2)}, u32[]{:S(2)}) %collective-permute-start.1) | collective-permute-done | bytes 40 | tf_op jit(solution)/shard_map/ppermute | solution.py:9
  253.1 0.8 broadcast_add_fusion
  253.9 0.0 slice-start
  253.9 0.1 broadcast_subtract_fusion
  253.9 0.0 slice-start.1
  253.9 0.0 copy-start.3
  254.0 0.0 collective-permute-done
  254.0 7.9 %fusion.2 = f32[4,128,4,512]{3,1,0,2:T(8,128)S(1)} fusion(bf16[4,512,2048]{2,1,0:T(8,128)(2,1)} %collective-permute-done, bf16[4,128,2048]{2,1,0:T(8,128)(2,1)} %param.3), kind=kOutput, calls=%fused_computation.2 | convolution fusion | flops 4294967296 | bytes 14680064 | tf_op jit(solution)/shard_map/dot_general | solution.py:13
  261.9 0.0 slice-done
  261.9 0.0 slice-done.1
  261.9 0.0 copy-done.3
  261.9 6.9 %fusion.13 = bf16[4,128,4,512]{3,1,0,2:T(8,128)(2,1)S(1)} fusion(f32[4,128,4,512]{3,1,0,2:T(8,128)S(1)} %fusion.2, bf16[4,512,2048]{2,1,0:T(8,128)(2,1)S(1)} %bitcast.76, f32[4,128,4]{1,0,2:T(4,128)S(1)} %get-tuple-element.5, bf16[4,512,2048]{2,1,0:T(8,128)(2,1)} %collective-permute-done, s32[]{:T(128)S(6)} %select_n.4, f32[512]{0:T(512)S(1)} %copy-done.3), kind=kOutput, calls=%fused_computation.15 | convolution fusion | flops 4300210176 | bytes 16787460 | tf_op jit(solution)/shard_map/dot_general | solution.py:13
  268.8 0.0 copy-start.1
  268.8 1.3 copy-done.1
  270.1 3.1 copy.16
  273.2 50.8 %all_to_all.15 = bf16[4,128,4,512]{1,0,2,3:T(4,128)(2,1)S(1)} all-to-all(bf16[4,128,4,512]{1,0,2,3:T(4,128)(2,1)} %copy.16), channel_id=1, replica_groups=mesh['copies'=2,'blk'=4,'virt'=4] {'virt'}, dimensions={3} | all-to-all | bytes 4194304 | tf_op jit(solution)/shard_map/all_to_all | solution.py:93
  324.0 3.1 copy.17
  327.1 2.0 copy.30
  329.0 2.4 copy.18
  331.4 0.0 copy-start
  331.4 8.7 %convolution_convert_fusion = bf16[4,128,2048]{2,1,0:T(8,128)(2,1)S(1)} fusion(bf16[4,128,2048]{2,1,0:T(8,128)(2,1)} %bitcast.73, bf16[2048,2048,1]{1,0,2:T(8,128)(2,1)} %bitcast.74), kind=kOutput, calls=%fused_computation.20 | convolution fusion | flops 4296015872 | bytes 12582912 | tf_op jit(solution)/shard_map/dot_general | solution.py:94
  340.0 2.2 collective-permute-start.2
  342.2 0.0 copy-done
  342.2 6.9 %fusion.8 = f32[4,128,4,512]{3,1,2,0:T(8,128)S(1)} fusion(bf16[4,512,2048]{2,1,0:T(8,128)(2,1)} %all-gather.2.cloned.1.call-done, bf16[4,128,2048]{2,1,0:T(8,128)(2,1)S(1)} %copy-done), kind=kOutput, calls=%fused_computation.8 | convolution fusion | flops 4294967296 | bytes 14680064 | tf_op jit(solution)/shard_map/dot_general | solution.py:13
  349.2 0.0 copy-start.2
  349.2 7.5 %fusion.4 = f32[4,128,2048,1]{2,1,0,3:T(8,128)S(1)} fusion(bf16[4,512,2048]{2,1,0:T(8,128)(2,1)} %all-gather.2.cloned.1.call-done, f32[4,128,4,512]{3,1,2,0:T(8,128)S(1)} %fusion.8, f32[512]{0:T(512)S(1)} %copy-done.3, f32[4,128,4]{1,0,2:T(4,128)S(1)} %get-tuple-element.6), kind=kOutput, calls=%fused_computation.4 | convolution fusion | flops 4300210176 | bytes 16787456 | tf_op jit(solution)/shard_map/dot_general | solution.py:52
  356.7 9.4 %collective-permute-done.2 = bf16[4,128,2048]{2,1,0:T(8,128)(2,1)S(1)} collective-permute-done((bf16[4,128,2048]{2,1,0:T(8,128)(2,1)S(1)}, bf16[4,128,2048]{2,1,0:T(8,128)(2,1)S(1)}, u32[]{:S(2)}, u32[]{:S(2)}) %collective-permute-start.2) | collective-permute-done | bytes 2097184 | tf_op jit(solution)/shard_map/ppermute | solution.py:9
  366.1 0.0 copy-done.2
  366.1 9.6 %fusion.11 = bf16[4,128,2048]{2,1,0:T(8,128)(2,1)} fusion(f32[4,128,2048,1]{2,1,0,3:T(8,128)S(1)} %fusion.4, bf16[4,128,2048]{2,1,0:T(8,128)(2,1)S(1)} %collective-permute-done.2, bf16[4,128,4,512]{3,1,0,2:T(8,128)(2,1)S(1)} %copy-done.2, bf16[4,512,2048]{2,1,0:T(8,128)(2,1)} %collective-permute-done), kind=kOutput, calls=%fused_computation.12 | convolution fusion | flops 4299161600 | bytes 18874368 | tf_op jit(solution)/shard_map/dot_general | solution.py:52
  (2 shorter events, 0.0 us)
Async XLA Ops:
  6.5 154.2 %all-gather.2.cloned.1.call-start = ((), (), s32[]{:S(2)}) async-start(), calls=%async_computation.1 | async-start | bytes 10485760 | tf_op jit(solution)/shard_map/all_gather | solution.py:65
  160.8 93.2 %collective-permute-start = (bf16[4,512,2048]{2,1,0:T(8,128)(2,1)}, bf16[4,512,2048]{2,1,0:T(8,128)(2,1)}, u32[]{:S(2)}, u32[]{:S(2)}) collective-permute-start(bf16[4,512,2048]{2,1,0:T(8,128)(2,1)} %all-gather.2.cloned.1.call-done), channel_id=1, source_target_pairs={{0,4},{4,8},{8,12},{12,0},{1,5},{5,9},{9,13},{13,1},{2,6},{6,10},{... | collective-permute-start | bytes 25165832 | tf_op jit(solution)/shard_map/ppermute | solution.py:9
  163.0 90.0 %collective-permute-start.1 = (bf16[4]{0:T(256)(128)(2,1)S(1)}, bf16[4]{0:T(256)(128)(2,1)S(1)}, u32[]{:S(2)}, u32[]{:S(2)}) collective-permute-start(bf16[4]{0:T(256)(128)(2,1)S(1)} %convert_element_type.22), channel_id=1, source_target_pairs={{0,4},{4,8},{8,12},{12,0},{1,5},{5,9},{9,13},{13,1},{2,6},{6,10},{... | collective-permute-start | bytes 32 | tf_op jit(solution)/shard_map/ppermute | solution.py:9
  253.9 8.0 %slice-start = ((s8[8388608]{0:T(1024)(128)(4,1)}), s8[4194304]{0:T(1024)(128)(4,1)S(1)}, s32[]{:S(2)}) async-start(s8[8388608]{0:T(1024)(128)(4,1)} %bitcast.75), calls=%async_computation.2 | async-start | bytes 8388608
  253.9 7.9 %slice-start.1 = ((s8[8388608]{0:T(1024)(128)(4,1)}), s8[4194304]{0:T(1024)(128)(4,1)S(1)}, s32[]{:S(2)}) async-start(s8[8388608]{0:T(1024)(128)(4,1)} %bitcast.75), calls=%async_computation.3 | async-start | bytes 8388608
  253.9 7.9 %copy-start.3 = (f32[512]{0:T(512)S(1)}, f32[512]{0:T(512)}, u32[]{:S(2)}) copy-start(f32[512]{0:T(512)} %param.5) | copy-start | bytes 6148
  268.8 1.3 copy-start.1
  331.4 10.8 %copy-start = (bf16[4,128,2048]{2,1,0:T(8,128)(2,1)S(1)}, bf16[4,128,2048]{2,1,0:T(8,128)(2,1)}, u32[]{:S(2)}) copy-start(bf16[4,128,2048]{2,1,0:T(8,128)(2,1)} %param.3) | copy-start | bytes 6291460
  340.0 26.1 %collective-permute-start.2 = (bf16[4,128,2048]{2,1,0:T(8,128)(2,1)S(1)}, bf16[4,128,2048]{2,1,0:T(8,128)(2,1)S(1)}, u32[]{:S(2)}, u32[]{:S(2)}) collective-permute-start(bf16[4,128,2048]{2,1,0:T(8,128)(2,1)S(1)} %convolution_convert_fusion), channel_id=1, source_target_pairs={{0,12},{4,0},{8,4},{12,8},{1,13},{5,1},{9,5},{13,9},{2,14},{6,2},{... | collective-permute-start | bytes 6291464 | tf_op jit(solution)/shard_map/ppermute | solution.py:9
  349.2 16.9 %copy-start.2 = (bf16[4,128,4,512]{3,1,0,2:T(8,128)(2,1)S(1)}, bf16[4,128,4,512]{3,1,0,2:T(8,128)(2,1)}, u32[]{:S(2)}) copy-start(bf16[4,128,4,512]{3,1,0,2:T(8,128)(2,1)} %copy-done.1) | copy-start | bytes 6291460
Sparse Core Ops, SparseCore 0:
  8.9 151.8 all-gather.1
where the time goes:
time: 383 us
  waiting for transfers between devices  253 us (66%)
  blocking collectives  50.8 us (13%)
  matrix products  47.5 us (12%)
  between operations  13.5 us (4%)
  local copies, waits for them, and re-layouts  12.6 us (3%)
    all_gather x1, waiting for transfers between devices, local(): own_full = lax.all_gather(three_index, 'virt', axis=1, tiled=True)  154 us
    ppermute x3, waiting for transfers between devices, shifted(): lax.ppermute(shard, axis, [(i, (i + by) % devices) for i in range(devices)])  98.7 us
    all_to_all x1, blocking collectives, local(): lax.all_to_all(tbar, 'virt', split_axis=3, concat_axis=1, tiled=True)  50.8 us
    dot_general x3, matrix products, contract(): lax.dot_general(left, right, (((1,), (1,)), ((), ())), preferred_element_...  21.7 us
    dot_general x2, matrix products, pair_block(): jnp.dot(flat, part_full.reshape(occ_count * virt_count, aux_count), prefe...  17.1 us
    dot_general x1, matrix products, local(): lax.dot_general(tiles.reshape(occ_count * virt_count, occ_count * rows_he...  8.65 us
  transfers between devices with their start and end apart: 4, of which 3 were waited for; matrix products, arithmetic and copies ran while one was open for 4% of the time, Pallas kernels for 0%

commit v1 on v0

--- a/solution.py
+++ b/solution.py
@@ -90,7 +90,10 @@
         virt_energy,
         False,
     )
-    tiles = lax.all_to_all(tbar, "virt", split_axis=3, concat_axis=1, tiled=True)
+    tiles = jnp.concatenate(
+        lax.all_to_all(jnp.stack(jnp.split(tbar, lax.axis_size("virt"), axis=3)), "virt", 0, 0),
+        axis=1,
+    )
     partial_value = lax.dot_general(
         tiles.reshape(occ_count * virt_count, occ_count * rows_here),
         own_full.reshape(occ_count * virt_count, aux_count),

time: 383 us -> 379 us (0.990)
  local copies, waits for them, and re-layouts: 12.6 us -> 6.32 us
where the time goes in v1:
time: 379 us; the launch traced here: 378 us
  waiting for transfers between devices  253 us (67%)
  matrix products  50.5 us (13%)
  blocking collectives  49.7 us (13%)
  between operations  13.5 us (4%)
  local copies, waits for them, and re-layouts  6.32 us (2%)
    all_gather x1, waiting for transfers between devices, local(): own_full = lax.all_gather(three_index, 'virt', axis=1, tiled=True)  154 us
    ppermute x3, waiting for transfers between devices, shifted(): lax.ppermute(shard, axis, [(i, (i + by) % devices) for i in range(devices)])  98.7 us
    all_to_all x1, blocking collectives, local(): lax.all_to_all(jnp.stack(jnp.split(tbar, lax.axis_size('virt'), axis=3)),...  49.7 us
    dot_general x3, matrix products, contract(): lax.dot_general(left, right, (((1,), (1,)), ((), ())), preferred_element_...  24.8 us
    dot_general x2, matrix products, pair_block(): jnp.dot(flat, part_full.reshape(occ_count * virt_count, aux_count), prefe...  17 us
    dot_general x1, matrix products, local(): lax.dot_general(tiles.reshape(occ_count * virt_count, occ_count * rows_he...  8.65 us
  transfers between devices with their start and end apart: 4, of which 3 were waited for; matrix products, arithmetic and copies ran while one was open for 4% of the time, Pallas kernels for 0%

profile of v1, /device:TPU:1, one launch (start us, length us, event | category | flops | bytes accessed | tf_op | source)
XLA Modules:
  0.0 378.4 jit_solution(13730529247134128544)
XLA Ops:
  6.5 0.0 all-gather.2.cloned.1.call-start
  6.5 0.7 all-gather.2.cloned.1.call-update
  7.3 153.5 %all-gather.2.cloned.1.call-done = bf16[4,512,2048]{2,1,0:T(8,128)(2,1)} async-done(((bf16[4,128,2048]{2,1,0:T(8,128)(2,1)}), bf16[4,512,2048]{2,1,0:T(8,128)(2,1)}) %all-gather.2.cloned.1.call-update) | async-done | bytes 8388624 | tf_op jit(solution)/shard_map/all_gather | solution.py:65
  160.8 1.6 collective-permute-start
  162.4 0.7 convert_element_type.22
  163.0 0.0 collective-permute-start.1
  163.0 0.8 dynamic_slice.6
  163.8 89.3 %collective-permute-done.1 = bf16[4]{0:T(256)(128)(2,1)S(1)} collective-permute-done((bf16[4]{0:T(256)(128)(2,1)S(1)}, bf16[4]{0:T(256)(128)(2,1)S(1)}, u32[]{:S(2)}, u32[]{:S(2)}) %collective-permute-start.1) | collective-permute-done | bytes 40 | tf_op jit(solution)/shard_map/ppermute | solution.py:9
  253.1 0.8 broadcast_add_fusion
  253.9 0.0 slice-start
  253.9 0.1 broadcast_subtract_fusion
  253.9 0.0 slice-start.1
  253.9 0.0 copy-start.3
  254.0 0.0 collective-permute-done
  254.0 10.7 %fusion.2 = f32[4,128,4,512]{3,1,0,2:T(8,128)} fusion(bf16[4,512,2048]{2,1,0:T(8,128)(2,1)} %collective-permute-done, bf16[4,128,2048]{2,1,0:T(8,128)(2,1)} %param.3), kind=kOutput, calls=%fused_computation.2 | convolution fusion | flops 4294967296 | bytes 14680064 | tf_op jit(solution)/shard_map/dot_general | solution.py:13
  264.6 0.0 slice-done
  264.6 0.0 slice-done.1
  264.6 0.0 copy-done.3
  264.6 7.2 %fusion.13 = bf16[4,128,4,512]{3,1,0,2:T(8,128)(2,1)S(1)} fusion(f32[4,128,4,512]{3,1,0,2:T(8,128)} %fusion.2, bf16[4,512,2048]{2,1,0:T(8,128)(2,1)S(1)} %bitcast.83, f32[4,128,4]{1,0,2:T(4,128)S(1)} %get-tuple-element.9, bf16[4,512,2048]{2,1,0:T(8,128)(2,1)} %collective-permute-done, s32[]{:T(128)S(6)} %select_n.4, f32[512]{0:T(512)S(1)} %copy-done.3), kind=kOutput, calls=%fused_computation.15 | convolution fusion | flops 4300210176 | bytes 16787460 | tf_op jit(solution)/shard_map/dot_general | solution.py:13
  271.9 0.0 copy-start.1
  271.9 0.6 slice_bitcast_fusion.3
  272.5 0.3 pad_maximum_fusion
  272.8 0.5 copy-done.1
  273.2 49.7 %all_to_all.5 = bf16[4,4,128,4,128]{4,2,1,3,0:T(8,128)(2,1)S(1)} all-to-all(bf16[4,4,128,4,128]{4,2,1,3,0:T(8,128)(2,1)S(1)} %pad_maximum_fusion), channel_id=1, replica_groups=mesh['copies'=2,'blk'=4,'virt'=4] {'virt'}, dimensions={0} | all-to-all | bytes 4194304 | tf_op jit(solution)/shard_map/all_to_all | solution.py:94
  322.9 1.8 copy.12
  324.7 0.4 copy.27
  325.0 2.4 copy.13
  327.4 0.0 copy-start
  327.4 8.7 %convolution_convert_fusion = bf16[4,128,2048]{2,1,0:T(8,128)(2,1)S(1)} fusion(bf16[4,128,2048]{2,1,0:T(8,128)(2,1)} %bitcast.80, bf16[2048,2048,1]{1,0,2:T(8,128)(2,1)} %bitcast.81), kind=kOutput, calls=%fused_computation.20 | convolution fusion | flops 4296015872 | bytes 12582912 | tf_op jit(solution)/shard_map/dot_general | solution.py:97
  336.1 2.0 collective-permute-start.2
  338.1 0.0 copy-done
  338.1 6.9 %fusion.8 = f32[4,128,4,512]{3,1,2,0:T(8,128)S(1)} fusion(bf16[4,512,2048]{2,1,0:T(8,128)(2,1)} %all-gather.2.cloned.1.call-done, bf16[4,128,2048]{2,1,0:T(8,128)(2,1)S(1)} %copy-done), kind=kOutput, calls=%fused_computation.8 | convolution fusion | flops 4294967296 | bytes 14680064 | tf_op jit(solution)/shard_map/dot_general | solution.py:13
  345.0 0.0 copy-start.2
  345.0 7.5 %fusion.4 = f32[4,128,2048,1]{2,1,0,3:T(8,128)S(1)} fusion(bf16[4,512,2048]{2,1,0:T(8,128)(2,1)} %all-gather.2.cloned.1.call-done, f32[4,128,4,512]{3,1,2,0:T(8,128)S(1)} %fusion.8, f32[512]{0:T(512)S(1)} %copy-done.3, f32[4,128,4]{1,0,2:T(4,128)S(1)} %get-tuple-element.10), kind=kOutput, calls=%fused_computation.4 | convolution fusion | flops 4300210176 | bytes 16787456 | tf_op jit(solution)/shard_map/dot_general | solution.py:52
  352.5 9.4 %collective-permute-done.2 = bf16[4,128,2048]{2,1,0:T(8,128)(2,1)S(1)} collective-permute-done((bf16[4,128,2048]{2,1,0:T(8,128)(2,1)S(1)}, bf16[4,128,2048]{2,1,0:T(8,128)(2,1)S(1)}, u32[]{:S(2)}, u32[]{:S(2)}) %collective-permute-start.2) | collective-permute-done | bytes 2097184 | tf_op jit(solution)/shard_map/ppermute | solution.py:9
  362.0 0.0 copy-done.2
  362.0 9.6 %fusion.11 = bf16[4,128,2048]{2,1,0:T(8,128)(2,1)} fusion(f32[4,128,2048,1]{2,1,0,3:T(8,128)S(1)} %fusion.4, bf16[4,128,2048]{2,1,0:T(8,128)(2,1)S(1)} %collective-permute-done.2, bf16[4,128,4,512]{3,1,0,2:T(8,128)(2,1)S(1)} %copy-done.2, bf16[4,512,2048]{2,1,0:T(8,128)(2,1)} %collective-permute-done), kind=kOutput, calls=%fused_computation.12 | convolution fusion | flops 4299161600 | bytes 18874368 | tf_op jit(solution)/shard_map/dot_general | solution.py:52
  (2 shorter events, 0.0 us)
Async XLA Ops:
  6.5 154.2 %all-gather.2.cloned.1.call-start = ((), (), s32[]{:S(2)}) async-start(), calls=%async_computation.1 | async-start | bytes 10485760 | tf_op jit(solution)/shard_map/all_gather | solution.py:65
  160.8 93.2 %collective-permute-start = (bf16[4,512,2048]{2,1,0:T(8,128)(2,1)}, bf16[4,512,2048]{2,1,0:T(8,128)(2,1)}, u32[]{:S(2)}, u32[]{:S(2)}) collective-permute-start(bf16[4,512,2048]{2,1,0:T(8,128)(2,1)} %all-gather.2.cloned.1.call-done), channel_id=1, source_target_pairs={{0,4},{4,8},{8,12},{12,0},{1,5},{5,9},{9,13},{13,1},{2,6},{6,10},{... | collective-permute-start | bytes 25165832 | tf_op jit(solution)/shard_map/ppermute | solution.py:9
  163.0 90.0 %collective-permute-start.1 = (bf16[4]{0:T(256)(128)(2,1)S(1)}, bf16[4]{0:T(256)(128)(2,1)S(1)}, u32[]{:S(2)}, u32[]{:S(2)}) collective-permute-start(bf16[4]{0:T(256)(128)(2,1)S(1)} %convert_element_type.22), channel_id=1, source_target_pairs={{0,4},{4,8},{8,12},{12,0},{1,5},{5,9},{9,13},{13,1},{2,6},{6,10},{... | collective-permute-start | bytes 32 | tf_op jit(solution)/shard_map/ppermute | solution.py:9
  253.9 10.8 %slice-start = ((s8[8388608]{0:T(1024)(128)(4,1)}), s8[4194304]{0:T(1024)(128)(4,1)S(1)}, s32[]{:S(2)}) async-start(s8[8388608]{0:T(1024)(128)(4,1)} %bitcast.82), calls=%async_computation.2 | async-start | bytes 8388608
  253.9 10.7 %slice-start.1 = ((s8[8388608]{0:T(1024)(128)(4,1)}), s8[4194304]{0:T(1024)(128)(4,1)S(1)}, s32[]{:S(2)}) async-start(s8[8388608]{0:T(1024)(128)(4,1)} %bitcast.82), calls=%async_computation.3 | async-start | bytes 8388608
  253.9 10.7 %copy-start.3 = (f32[512]{0:T(512)S(1)}, f32[512]{0:T(512)}, u32[]{:S(2)}) copy-start(f32[512]{0:T(512)} %param.5) | copy-start | bytes 6148
  271.9 1.3 copy-start.1
  327.4 10.7 %copy-start = (bf16[4,128,2048]{2,1,0:T(8,128)(2,1)S(1)}, bf16[4,128,2048]{2,1,0:T(8,128)(2,1)}, u32[]{:S(2)}) copy-start(bf16[4,128,2048]{2,1,0:T(8,128)(2,1)} %param.3) | copy-start | bytes 6291460
  336.1 25.9 %collective-permute-start.2 = (bf16[4,128,2048]{2,1,0:T(8,128)(2,1)S(1)}, bf16[4,128,2048]{2,1,0:T(8,128)(2,1)S(1)}, u32[]{:S(2)}, u32[]{:S(2)}) collective-permute-start(bf16[4,128,2048]{2,1,0:T(8,128)(2,1)S(1)} %convolution_convert_fusion), channel_id=1, source_target_pairs={{0,12},{4,0},{8,4},{12,8},{1,13},{5,1},{9,5},{13,9},{2,14},{6,2},{... | collective-permute-start | bytes 6291464 | tf_op jit(solution)/shard_map/ppermute | solution.py:9
  345.0 16.9 %copy-start.2 = (bf16[4,128,4,512]{3,1,0,2:T(8,128)(2,1)S(1)}, bf16[4,128,4,512]{3,1,0,2:T(8,128)(2,1)}, u32[]{:S(2)}) copy-start(bf16[4,128,4,512]{3,1,0,2:T(8,128)(2,1)} %copy-done.1) | copy-start | bytes 6291460
Sparse Core Ops, SparseCore 0:
  8.9 151.8 all-gather.1
